TPU v7x, 256 devices: a whole 4x4x8 slice. The times are simulated.
256 devices in a mesh: rep: 8 (over y_lo, x), seq: 32 (over y_hi, z, core).
Axes of the slice: x: 4, y: 4 (y_hi: 2, y_lo: 2; y = y_hi * 2 + y_lo), z: 8, core: 2. Of those that a mesh axis runs over, the one named last changes fastest.
Arguments:
- queries: bfloat16 [8, 4096, 3072], P('rep', 'seq'), may hold values from -6 to 6
- keys: bfloat16 [8, 4096, 128], P('rep', 'seq'), may hold values from -6 to 6
- values: bfloat16 [8, 4096, 128], P('rep', 'seq'), may hold values from -6 to 6
- outputs: bfloat16 [8, 4096, 3072], P('rep', 'seq'), may hold values from -6 to 6
- out_grad: bfloat16 [8, 4096, 3072], P('rep', 'seq'), may hold values from -24 to 24
- log_norm: float32 [8, 24, 4096], P('rep', None, 'seq'), may hold values from 7 to 8.5
- inputs: bfloat16 [8, 4096, 6144], P('rep', 'seq'), may hold values from -0.29882812 to 0.29882812
- mlp_weight: bfloat16 [8, 12288, 6144], P('rep', 'seq'), may hold values from -0.0546875 to 0.0546875
- initial_right_factor: bfloat16 [32, 4, 6144], P('seq'), may hold values from -6 to 6
Outputs:
- query_grad: float32 [8, 4096, 3072], P('rep', 'seq')
- kv_grad: float32 [8, 4096, 256], P('rep', 'seq')
- proj_grad: float32 [8, 6144, 256], P('rep', 'seq')
- left_factor: float32 [8, 2, 4, 12288], P('rep', None, None, 'seq')
- right_factor: float32 [8, 32, 2, 4, 6144], P('rep', 'seq')
All inputs are finite; a program needn't handle non-finite values.
Results may differ from a plain program's by a relative error of at most 0.004.
Values may be sent and summed in bfloat16 or wider, within the bound.
A program may use at most 128 MiB of HBM per device.

v0:
```python
import jax
import jax.numpy as jnp
from jax import lax
from jax.sharding import PartitionSpec as P

WINDOW = 2048


epsilon = 1e-06


def shifted(block, axis, distance):
    devices = range(lax.axis_size(axis))
    route = [(i - distance, i) for i in devices if i - distance in devices]
    return lax.ppermute(block, axis, route)


def extended(block, sides, width):
    for axis, dim in sides:
        count = lax.axis_size(axis)
        forward = [(i, i + 1) for i in range(count - 1)]
        forward.append((count - 1, 0))
        backward = [(target, source) for source, target in forward]
        low = lax.ppermute(
            lax.slice_in_dim(block, block.shape[dim] - width, None, axis=dim), axis, forward
        )
        high = lax.ppermute(lax.slice_in_dim(block, 0, width, axis=dim), axis, backward)
        block = jnp.concatenate([low, block, high], axis=dim)
    return block


def window_mask(first_query, row_count, span):
    query_pos = first_query + jnp.arange(row_count, dtype=jnp.int32)
    key_pos = first_query - span + jnp.arange(span + row_count, dtype=jnp.int32)
    lower_ok = key_pos[None, :] > query_pos[:, None] - span
    upper_ok = key_pos[None, :] <= query_pos[:, None]
    return (key_pos[None, :] >= 0) & lower_ok & upper_ok


def attend(query_blk, gradient_block, out_blk, norm_block, window_kv, visible, scale):
    row_count, model_cols = query_blk.shape
    head_count = norm_block.shape[0]
    width = model_cols // head_count
    group = 8
    groups = head_count // group

    def head_rows(source):
        return (
            source.reshape(row_count, head_count, width)
            .transpose(1, 0, 2)
            .reshape(groups, group * row_count, width)
        )

    query_rows = head_rows(query_blk)
    grad_rows = head_rows(gradient_block)
    delta_all = jnp.sum(
        gradient_block.astype(jnp.float32).reshape(row_count, head_count, width)
        * out_blk.astype(jnp.float32).reshape(row_count, head_count, width),
        axis=-1,
    )
    delta_rows = delta_all.T.reshape(groups, group * row_count)
    norm_rows = norm_block.reshape(groups, group, row_count)
    key_mat = window_kv[:, :width]
    value_mat = window_kv[:, width:]

    def per_group(accum, items):
        query_grp, grad_grp, norm_grp, delta_grp = items
        scores = jnp.dot(query_grp, key_mat.T, preferred_element_type=jnp.float32) * scale
        scores = scores.reshape(group, row_count, -1)
        probs = jnp.where(visible[None], jnp.exp(scores - norm_grp[:, :, None]), 0.0)
        probs = probs.reshape(group * row_count, -1)
        probs_b = probs.astype(jnp.bfloat16)
        value_grad = jnp.dot(probs_b.T, grad_grp, preferred_element_type=jnp.float32)
        prob_grad = jnp.dot(grad_grp, value_mat.T, preferred_element_type=jnp.float32)
        score_grad = (scale * probs * (prob_grad - delta_grp[:, None])).astype(jnp.bfloat16)
        query_grad = jnp.dot(score_grad, key_mat, preferred_element_type=jnp.float32)
        key_grad = jnp.dot(score_grad.T, query_grp, preferred_element_type=jnp.float32)
        return (accum + jnp.concatenate([key_grad, value_grad], axis=-1), query_grad)

    start_accum = jnp.zeros((window_kv.shape[0], 2 * width), jnp.float32)
    accum, query_grads = lax.scan(
        per_group, start_accum, (query_rows, grad_rows, norm_rows, delta_rows)
    )
    query_grad = (
        query_grads.reshape(head_count, row_count, width)
        .transpose(1, 0, 2)
        .reshape(row_count, model_cols)
    )
    return (query_grad, accum)


def orthonormal(diffs):
    columns = []
    for index in range(diffs.shape[-2]):
        source = diffs[..., index, :]
        vector = source
        for previous in columns:
            vector = vector - jnp.mean(source * previous, axis=-1, keepdims=True) * previous
        columns.append(
            vector * lax.rsqrt(jnp.mean(vector * vector, axis=-1, keepdims=True) + epsilon)
        )
    return jnp.stack(columns, axis=-2)


def on_device(
    queries, keys, values, outputs, out_grad, log_norm, inputs, mlp_weight, initial_right_factor
):
    tok_rows = queries.shape[1]
    head_dim = keys.shape[2]
    own_kv = jnp.concatenate([keys[0], values[0]], axis=-1)
    span_blocks = WINDOW // tok_rows
    level_count = span_blocks.bit_length() - 1
    earlier_kv = own_kv
    for level_index in range(level_count + 1):
        payload = own_kv if level_index == 0 else earlier_kv
        distance = 1 if level_index == 0 else earlier_kv.shape[0] // tok_rows
        arrived = shifted(payload, "seq", distance)
        earlier_kv = arrived if level_index == 0 else jnp.concatenate([arrived, earlier_kv], axis=0)
    window_kv = jnp.concatenate([earlier_kv, own_kv], axis=0)
    first_query = lax.axis_index("seq") * tok_rows
    visible = window_mask(first_query, tok_rows, WINDOW)
    query_grad, window_grads = attend(
        queries[0], out_grad[0], outputs[0], log_norm[0], window_kv, visible, head_dim ** (-0.5)
    )
    remaining = window_grads[:WINDOW]
    own_grad = window_grads[WINDOW:]
    for level_index in range(level_count + 1):
        if level_index < level_count:
            half_rows = remaining.shape[0] // 2
            send_part = remaining[:half_rows]
            kept_part = remaining[half_rows:]
            distance = half_rows // tok_rows
        else:
            send_part = remaining
            kept_part = remaining
            distance = 1
        returned = shifted(send_part, "seq", -distance)
        if level_index < level_count:
            remaining = kept_part + returned
        else:
            own_grad = own_grad + returned
    kv_grad_b = own_grad.astype(jnp.bfloat16)
    input_local = inputs[0]
    proj_grad = lax.psum_scatter(
        jnp.dot(input_local.T, kv_grad_b, preferred_element_type=jnp.float32),
        "seq",
        scatter_dimension=0,
        tiled=True,
    )
    weight_block = mlp_weight[0]
    acts = jnp.einsum(
        "kd,rd->kr", initial_right_factor[0], weight_block, preferred_element_type=jnp.float32
    )
    cycle_acts = extended(acts[None], (("rep", 0),), 1)
    diffs = jnp.stack([acts - cycle_acts[0], acts - cycle_acts[2]], axis=0)
    basis = orthonormal(diffs)
    contrib = jnp.einsum(
        "ekr,rd->ekd", basis.astype(jnp.bfloat16), weight_block, preferred_element_type=jnp.float32
    )
    cycle_contrib = extended(contrib, (("rep", 0),), 1)
    right_factor = jnp.stack([contrib[0] + cycle_contrib[0], contrib[1] + cycle_contrib[3]], axis=0)
    return (
        query_grad[None],
        own_grad[None],
        proj_grad[None],
        basis[None],
        right_factor[None, None],
    )


def solution(mesh):
    return jax.shard_map(
        on_device,
        mesh=mesh,
        in_specs=(
            P("rep", "seq", None),
            P("rep", "seq", None),
            P("rep", "seq", None),
            P("rep", "seq", None),
            P("rep", "seq", None),
            P("rep", None, "seq"),
            P("rep", "seq", None),
            P("rep", "seq", None),
            P("seq", None, None),
        ),
        out_specs=(
            P("rep", "seq", None),
            P("rep", "seq", None),
            P("rep", "seq", None),
            P("rep", None, None, "seq"),
            P("rep", "seq", None, None, None),
        ),
        check_vma=False,
    )
```

profile of v0, /device:TPU:1, one launch (start us, length us, event | category | flops | bytes accessed | tf_op | source)
XLA Modules:
  0.0 385.7 jit_solution(2791320941173070438)
XLA Ops:
  8.1 4.9 %collective-permute-start = (bf16[128,256]{1,0:T(8,128)(2,1)S(1)}, bf16[128,256]{1,0:T(8,128)(2,1)S(1)}, u32[]{:S(2)}, u32[]{:S(2)}) collective-permute-start(bf16[128,256]{1,0:T(8,128)(2,1)S(1)} %pad_maximum_fusion.3), channel_id=1, source_target_pairs={{0,1},{1,2},{2,3},{3,4},{4,5},{5,6},{6,7},{7,8},{8,9},{9,10},{10,1... | collective-permute-start | bytes 196616 | tf_op jit(solution)/shard_map/ppermute | solution.py:15
  14.4 4.3 %collective-permute-start.1 = (bf16[128,256]{1,0:T(8,128)(2,1)S(1)}, bf16[128,256]{1,0:T(8,128)(2,1)S(1)}, u32[]{:S(2)}, u32[]{:S(2)}) collective-permute-start(bf16[128,256]{1,0:T(8,128)(2,1)S(1)} %collective-permute-done), channel_id=1, source_target_pairs={{0,1},{1,2},{2,3},{3,4},{4,5},{5,6},{6,7},{7,8},{8,9},{9,10},{10,1... | collective-permute-start | bytes 196616 | tf_op jit(solution)/shard_map/ppermute | solution.py:15
  19.9 3.5 collective-permute-start.2
  26.4 7.3 %collective-permute-start.3 = (bf16[512,256]{1,0:T(8,128)(2,1)S(1)}, bf16[512,256]{1,0:T(8,128)(2,1)S(1)}, u32[]{:S(2)}, u32[]{:S(2)}) collective-permute-start(bf16[512,256]{1,0:T(8,128)(2,1)S(1)} %pad_maximum_fusion.1), channel_id=1, source_target_pairs={{0,4},{1,5},{2,6},{3,7},{4,8},{5,9},{6,10},{7,11},{8,12},{9,13},{1... | collective-permute-start | bytes 786440 | tf_op jit(solution)/shard_map/ppermute | solution.py:15
  34.2 7.9 %collective-permute-done.3 = bf16[512,256]{1,0:T(8,128)(2,1)S(1)} collective-permute-done((bf16[512,256]{1,0:T(8,128)(2,1)S(1)}, bf16[512,256]{1,0:T(8,128)(2,1)S(1)}, u32[]{:S(2)}, u32[]{:S(2)}) %collective-permute-start.3) | collective-permute-done | bytes 262176 | tf_op jit(solution)/shard_map/ppermute | solution.py:15
  42.9 6.3 %collective-permute-start.4 = (bf16[1024,256]{1,0:T(8,128)(2,1)}, bf16[1024,256]{1,0:T(8,128)(2,1)S(1)}, u32[]{:S(2)}, u32[]{:S(2)}) collective-permute-start(bf16[1024,256]{1,0:T(8,128)(2,1)} %pad_maximum_fusion), channel_id=1, source_target_pairs={{0,8},{1,9},{2,10},{3,11},{4,12},{5,13},{6,14},{7,15},{8,16},{9,17... | collective-permute-start | bytes 1572872 | tf_op jit(solution)/shard_map/ppermute | solution.py:15
  50.9 19.0 %collective-permute-done.4 = bf16[1024,256]{1,0:T(8,128)(2,1)S(1)} collective-permute-done((bf16[1024,256]{1,0:T(8,128)(2,1)}, bf16[1024,256]{1,0:T(8,128)(2,1)S(1)}, u32[]{:S(2)}, u32[]{:S(2)}) %collective-permute-start.4) | collective-permute-done | bytes 524320 | tf_op jit(solution)/shard_map/ppermute | solution.py:15
  70.2 50.5 %while.13 = (s32[]{:T(128)}, f32[2176,256]{0,1:T(8,128)}, f32[3,1024,128]{2,1,0:T(8,128)}, bf16[3,1024,128]{2,1,0:T(8,128)(2,1)S(1)}, bf16[2176,128]{1,0:T(8,128...) while((s32[]{:T(128)}, f32[2176,256]{0,1:T(8,128)}, ...), condition=%wide.region_2.3_spmd.clone, body=%wide.region_1.2_spmd.clone.sunk | while | flops 2872737792 | bytes 102404104 | solution.py:81
  83.3 3.3 fusion.81
  96.6 3.8 maximum_add_fusion.2
  100.3 3.3 fusion.81
  113.6 3.8 maximum_add_fusion.2
  117.4 3.3 fusion.81
  126.3 29.7 %collective-permute-done.5 = f32[1024,256]{1,0:T(8,128)S(1)} collective-permute-done((f32[1024,256]{1,0:T(8,128)S(1)}, f32[1024,256]{1,0:T(8,128)S(1)}, u32[]{:S(2)}, u32[]{:S(2)}) %collective-permute-start.5) | collective-permute-done | bytes 1048608 | tf_op jit(solution)/shard_map/ppermute | solution.py:15
  158.7 29.2 %collective-permute-done.6 = f32[512,256]{1,0:T(8,128)S(1)} collective-permute-done((f32[512,256]{1,0:T(8,128)S(1)}, f32[512,256]{1,0:T(8,128)S(1)}, u32[]{:S(2)}, u32[]{:S(2)}) %collective-permute-start.6) | collective-permute-done | bytes 524320 | tf_op jit(solution)/shard_map/ppermute | solution.py:15
  189.3 21.8 %collective-permute-done.7 = f32[256,256]{1,0:T(8,128)S(1)} collective-permute-done((f32[256,256]{1,0:T(8,128)S(1)}, f32[256,256]{1,0:T(8,128)S(1)}, u32[]{:S(2)}, u32[]{:S(2)}) %collective-permute-start.7) | collective-permute-done | bytes 262176 | tf_op jit(solution)/shard_map/ppermute | solution.py:15
  211.2 3.7 collective-permute-start.8
  214.9 4.0 %collective-permute-done.8 = f32[128,256]{1,0:T(8,128)S(1)} collective-permute-done((f32[128,256]{1,0:T(8,128)S(1)}, f32[128,256]{1,0:T(8,128)S(1)}, u32[]{:S(2)}, u32[]{:S(2)}) %collective-permute-start.8) | collective-permute-done | bytes 131104 | tf_op jit(solution)/shard_map/ppermute | solution.py:15
  221.0 4.2 %collective-permute-done.9 = f32[128,256]{1,0:T(8,128)S(1)} collective-permute-done((f32[128,256]{1,0:T(8,128)S(1)}, f32[128,256]{1,0:T(8,128)S(1)}, u32[]{:S(2)}, u32[]{:S(2)}) %collective-permute-start.9) | collective-permute-done | bytes 131104 | tf_op jit(solution)/shard_map/ppermute | solution.py:15
  225.1 4.5 %convolution_bitcast_fusion.1 = f32[6144,256]{0,1:T(8,128)} fusion(bf16[1,128,6144]{2,1,0:T(8,128)(2,1)S(1)} %copy-done, f32[128,256]{1,0:T(8,128)S(1)} %collective-permute-done.9, f32[2176,256]{1,0:T(8,128)} %copy.52), kind=kOutput, calls=%fused_computation.24 | convolution fusion | flops 402718720 | bytes 8126464 | tf_op jit(solution)/shard_map/dot_general | solution.py:145
  229.7 6.6 %copy.59 = f32[6144,256]{1,0:T(8,128)} copy(f32[6144,256]{0,1:T(8,128)} %convolution_bitcast_fusion.1) | data formatting | bytes 12582912
  237.1 3.6 fusion.20
  250.5 3.4 collective-permute-start.13
  260.4 116.6 %reduce-scatter.4.cloned.1.call-done = f32[192,256]{1,0:T(8,128)} async-done(((f32[6144,256]{1,0:T(8,128)}), f32[192,256]{1,0:T(8,128)}) %reduce-scatter.4.cloned.1.call-update) | async-done | bytes 196624
  (159 shorter events, 73.1 us)
Async XLA Ops:
  7.2 218.0 %copy-start = (bf16[1,128,6144]{2,1,0:T(8,128)(2,1)S(1)}, bf16[1,128,6144]{2,1,0:T(8,128)(2,1)}, u32[]{:S(2)}) copy-start(bf16[1,128,6144]{2,1,0:T(8,128)(2,1)} %param.17) | copy-start | bytes 4718596
  7.2 369.8 %reduce-scatter.4.cloned.1.call-start = ((), (), s32[]{:S(2)}) async-start(), calls=%async_computation.1 | async-start | bytes 6488064
  8.1 6.2 %collective-permute-start = (bf16[128,256]{1,0:T(8,128)(2,1)S(1)}, bf16[128,256]{1,0:T(8,128)(2,1)S(1)}, u32[]{:S(2)}, u32[]{:S(2)}) collective-permute-start(bf16[128,256]{1,0:T(8,128)(2,1)S(1)} %pad_maximum_fusion.3), channel_id=1, source_target_pairs={{0,1},{1,2},{2,3},{3,4},{4,5},{5,6},{6,7},{7,8},{8,9},{9,10},{10,1... | collective-permute-start | bytes 196616 | tf_op jit(solution)/shard_map/ppermute | solution.py:15
  14.4 5.6 %collective-permute-start.1 = (bf16[128,256]{1,0:T(8,128)(2,1)S(1)}, bf16[128,256]{1,0:T(8,128)(2,1)S(1)}, u32[]{:S(2)}, u32[]{:S(2)}) collective-permute-start(bf16[128,256]{1,0:T(8,128)(2,1)S(1)} %collective-permute-done), channel_id=1, source_target_pairs={{0,1},{1,2},{2,3},{3,4},{4,5},{5,6},{6,7},{7,8},{8,9},{9,10},{10,1... | collective-permute-start | bytes 196616 | tf_op jit(solution)/shard_map/ppermute | solution.py:15
  19.9 6.5 %collective-permute-start.2 = (bf16[256,256]{1,0:T(8,128)(2,1)S(1)}, bf16[256,256]{1,0:T(8,128)(2,1)S(1)}, u32[]{:S(2)}, u32[]{:S(2)}) collective-permute-start(bf16[256,256]{1,0:T(8,128)(2,1)S(1)} %pad_maximum_fusion.2), channel_id=1, source_target_pairs={{0,2},{1,3},{2,4},{3,5},{4,6},{5,7},{6,8},{7,9},{8,10},{9,11},{10,... | collective-permute-start | bytes 393224 | tf_op jit(solution)/shard_map/ppermute | solution.py:15
  25.1 8.7 %copy-start.10 = (bf16[1,128,3072]{2,1,0:T(8,128)(2,1)S(1)}, bf16[1,128,3072]{2,1,0:T(8,128)(2,1)}, u32[]{:S(2)}) copy-start(bf16[1,128,3072]{2,1,0:T(8,128)(2,1)} %param.14) | copy-start | bytes 2359300
  26.4 15.6 %collective-permute-start.3 = (bf16[512,256]{1,0:T(8,128)(2,1)S(1)}, bf16[512,256]{1,0:T(8,128)(2,1)S(1)}, u32[]{:S(2)}, u32[]{:S(2)}) collective-permute-start(bf16[512,256]{1,0:T(8,128)(2,1)S(1)} %pad_maximum_fusion.1), channel_id=1, source_target_pairs={{0,4},{1,5},{2,6},{3,7},{4,8},{5,9},{6,10},{7,11},{8,12},{9,13},{1... | collective-permute-start | bytes 786440 | tf_op jit(solution)/shard_map/ppermute | solution.py:15
  42.9 27.0 %collective-permute-start.4 = (bf16[1024,256]{1,0:T(8,128)(2,1)}, bf16[1024,256]{1,0:T(8,128)(2,1)S(1)}, u32[]{:S(2)}, u32[]{:S(2)}) collective-permute-start(bf16[1024,256]{1,0:T(8,128)(2,1)} %pad_maximum_fusion), channel_id=1, source_target_pairs={{0,8},{1,9},{2,10},{3,11},{4,12},{5,13},{6,14},{7,15},{8,16},{9,17... | collective-permute-start | bytes 1572872 | tf_op jit(solution)/shard_map/ppermute | solution.py:15
  49.2 20.9 %copy-start.11 = (bf16[1,128,128]{2,1,0:T(8,128)(2,1)S(1)}, bf16[1,128,128]{2,1,0:T(8,128)(2,1)}, u32[]{:S(2)}) copy-start(bf16[1,128,128]{2,1,0:T(8,128)(2,1)} %param.13) | copy-start | bytes 98308
  49.2 20.9 %copy-start.12 = (bf16[1,128,128]{2,1,0:T(8,128)(2,1)S(1)}, bf16[1,128,128]{2,1,0:T(8,128)(2,1)}, u32[]{:S(2)}) copy-start(bf16[1,128,128]{2,1,0:T(8,128)(2,1)} %param.12) | copy-start | bytes 98308
  70.2 4.0 %copy-start.3 = (bf16[2176,128]{1,0:T(8,128)(2,1)}, bf16[2176,128]{1,0:T(8,128)(2,1)S(1)}, u32[]{:S(2)}) copy-start(bf16[2176,128]{1,0:T(8,128)(2,1)S(1)} %get-tuple-element.299) | copy-start | bytes 1671172 | tf_op jit(solution)/shard_map/while
  70.2 4.0 %copy-start.6 = (bf16[3,1024,128]{2,1,0:T(8,128)(2,1)}, bf16[3,1024,128]{2,1,0:T(8,128)(2,1)S(1)}, u32[]{:S(2)}) copy-start(bf16[3,1024,128]{2,1,0:T(8,128)(2,1)S(1)} %get-tuple-element.298) | copy-start | bytes 2359300 | tf_op jit(solution)/shard_map/while
  86.6 4.0 %copy-start.6 = (bf16[3,1024,128]{2,1,0:T(8,128)(2,1)}, bf16[3,1024,128]{2,1,0:T(8,128)(2,1)S(1)}, u32[]{:S(2)}) copy-start(bf16[3,1024,128]{2,1,0:T(8,128)(2,1)S(1)} %get-tuple-element.298) | copy-start | bytes 2359300 | tf_op jit(solution)/shard_map/while
  103.6 4.0 %copy-start.6 = (bf16[3,1024,128]{2,1,0:T(8,128)(2,1)}, bf16[3,1024,128]{2,1,0:T(8,128)(2,1)S(1)}, u32[]{:S(2)}) copy-start(bf16[3,1024,128]{2,1,0:T(8,128)(2,1)S(1)} %get-tuple-element.298) | copy-start | bytes 2359300 | tf_op jit(solution)/shard_map/while
  125.0 31.0 %collective-permute-start.5 = (f32[1024,256]{1,0:T(8,128)S(1)}, f32[1024,256]{1,0:T(8,128)S(1)}, u32[]{:S(2)}, u32[]{:S(2)}) collective-permute-start(f32[1024,256]{1,0:T(8,128)S(1)} %slice.77), channel_id=1, source_target_pairs={{8,0},{9,1},{10,2},{11,3},{12,4},{13,5},{14,6},{15,7},{16,8},{17,9... | collective-permute-start | bytes 3145736 | tf_op jit(solution)/shard_map/ppermute | solution.py:15
  157.4 30.5 %collective-permute-start.6 = (f32[512,256]{1,0:T(8,128)S(1)}, f32[512,256]{1,0:T(8,128)S(1)}, u32[]{:S(2)}, u32[]{:S(2)}) collective-permute-start(f32[512,256]{1,0:T(8,128)S(1)} %slice.79), channel_id=1, source_target_pairs={{4,0},{5,1},{6,2},{7,3},{8,4},{9,5},{10,6},{11,7},{12,8},{13,9},{1... | collective-permute-start | bytes 1572872 | tf_op jit(solution)/shard_map/ppermute | solution.py:15
  188.0 23.1 %collective-permute-start.7 = (f32[256,256]{1,0:T(8,128)S(1)}, f32[256,256]{1,0:T(8,128)S(1)}, u32[]{:S(2)}, u32[]{:S(2)}) collective-permute-start(f32[256,256]{1,0:T(8,128)S(1)} %slice.81), channel_id=1, source_target_pairs={{2,0},{3,1},{4,2},{5,3},{6,4},{7,5},{8,6},{9,7},{10,8},{11,9},{12,... | collective-permute-start | bytes 786440 | tf_op jit(solution)/shard_map/ppermute | solution.py:15
  211.2 7.6 %collective-permute-start.8 = (f32[128,256]{1,0:T(8,128)S(1)}, f32[128,256]{1,0:T(8,128)S(1)}, u32[]{:S(2)}, u32[]{:S(2)}) collective-permute-start(f32[128,256]{1,0:T(8,128)S(1)} %slice.83), channel_id=1, source_target_pairs={{1,0},{2,1},{3,2},{4,3},{5,4},{6,5},{7,6},{8,7},{9,8},{10,9},{11,1... | collective-permute-start | bytes 393224 | tf_op jit(solution)/shard_map/ppermute | solution.py:15
  218.9 6.3 %collective-permute-start.9 = (f32[128,256]{1,0:T(8,128)S(1)}, f32[128,256]{1,0:T(8,128)S(1)}, u32[]{:S(2)}, u32[]{:S(2)}) collective-permute-start(f32[128,256]{1,0:T(8,128)S(1)} %slice_add_fusion.3), channel_id=1, source_target_pairs={{1,0},{2,1},{3,2},{4,3},{5,4},{6,5},{7,6},{8,7},{9,8},{10,9},{11,1... | collective-permute-start | bytes 393224 | tf_op jit(solution)/shard_map/ppermute | solution.py:15
  240.7 4.6 %collective-permute-start.10 = (f32[1,4,384]{2,1,0:T(4,128)S(1)}, f32[1,4,384]{2,1,0:T(4,128)S(1)}, u32[]{:S(2)}, u32[]{:S(2)}) collective-permute-start(f32[1,4,384]{2,1,0:T(4,128)S(1)} %bitcast.178), channel_id=1, source_target_pairs={{0,32},{32,64},{64,96},{96,128},{128,160},{160,192},{192,224},{224... | collective-permute-start | bytes 18440 | tf_op jit(solution)/shard_map/ppermute | solution.py:24
  241.9 3.4 collective-permute-start.11
  246.9 9.7 %copy-start.8 = (f32[3,1024,128]{2,1,0:T(8,128)S(1)}, f32[3,1024,128]{2,1,0:T(8,128)}, u32[]{:S(2)}) copy-start(f32[3,1024,128]{2,1,0:T(8,128)} %get-tuple-element.58) | copy-start | bytes 4718596
  250.1 5.7 %collective-permute-start.12 = (f32[1,4,6144]{2,1,0:T(4,128)S(1)}, f32[1,4,6144]{2,1,0:T(4,128)S(1)}, u32[]{:S(2)}, u32[]{:S(2)}) collective-permute-start(f32[1,4,6144]{2,1,0:T(4,128)S(1)} %get-tuple-element.176), channel_id=1, source_target_pairs={{0,32},{32,64},{64,96},{96,128},{128,160},{160,192},{192,224},{224... | collective-permute-start | bytes 294920 | tf_op jit(solution)/shard_map/ppermute | solution.py:24
  250.5 5.3 %collective-permute-start.13 = (f32[1,4,6144]{2,1,0:T(4,128)S(1)}, f32[1,4,6144]{2,1,0:T(4,128)S(1)}, u32[]{:S(2)}, u32[]{:S(2)}) collective-permute-start(f32[1,4,6144]{2,1,0:T(4,128)S(1)} %get-tuple-element.177), channel_id=1, source_target_pairs={{32,0},{64,32},{96,64},{128,96},{160,128},{192,160},{224,192},{0,2... | collective-permute-start | bytes 294920 | tf_op jit(solution)/shard_map/ppermute | solution.py:27
  (19 other events, 56.2 us)
Sparse Core Ops, SparseCore 0:
  236.4 140.5 reduce-scatter.3
where the time goes:
time: 390 us; the launch traced here: 386 us
  waiting for transfers between devices  237 us (61%)
  matrix products  43.5 us (11%)
  starting transfers between devices  43.3 us (11%)
  local copies, waits for them, and re-layouts  24.9 us (6%)
  other arithmetic  21.9 us (6%)
  between operations  14.5 us (4%)
    ppermute x10, waiting for transfers between devices, shifted(): return lax.ppermute(block, axis, route)  118 us
    unnamed x2, waiting for transfers between devices  117 us
    ppermute x10, starting transfers between devices, shifted(): return lax.ppermute(block, axis, route)  36 us
    unnamed x26, local copies, waits for them, and re-layouts  11.7 us
    add x3, other arithmetic, per_group(): accum + jnp.concatenate([key_grad, value_grad], axis=-1)  10.6 us
    dot_general x3, matrix products, per_group(): jnp.dot(score_grad, key_mat, preferred_element_type=jnp.float32)  9.83 us
    dot_general x3, matrix products, per_group(): jnp.dot(score_grad.T, query_grp, preferred_element_type=jnp.float32)  8.88 us
  transfers between devices with their start and end apart: 15, of which 12 were waited for; matrix products, arithmetic and copies ran while one was open for 5% of the time, Pallas kernels for 0%

commit v1 on v0

v1 whole, which is shorter than its diff:
```python
import functools

import jax
import jax.numpy as jnp
from jax import lax
from jax.experimental import pallas as pl
from jax.experimental.pallas import tpu as pltpu
from jax.sharding import PartitionSpec as P

MESH = pl.DeviceIdType.MESH
F32 = jnp.float32
BF16 = jnp.bfloat16
EPS = 1e-06
NT = (((1,), (1,)), ((), ()))

HD = 128
HEADS = 24
TOK = 128
SPAN = 8
ROWS = 384
HALF = 192
WINDOW = 2048


def kernel(
    q_hbm, k_hbm, v_hbm, o_hbm, g_hbm, lse_hbm, x_hbm, w_hbm, f_hbm,
    dq_out, kv_out, proj_out, left_out, right_out,
    q_in, g_in, o_in, lse_in, w_in, f_in,
    q_rows, g_rows, q_cols, g_cols, lse_b, delta_b, dq_acc, bias,
    kv_buf, part, pin, gsend, grecv, own, x_all, kg, psend, precv,
    acts, acts_in, contrib, contrib_in,
    load_sem, kv_s, kv_r, fw_s, fw_r, pt_s, pt_r, gr_s, gr_r,
    x_s, x_r, kg_s, kg_r, pr_s, pr_r, a_s, a_r, c_s, c_r, dq_s,
):
    rep = lax.axis_index("rep")
    seq = lax.axis_index("seq")
    core = seq % 2
    chip = seq // 2
    half = chip // 8
    zpos = chip % 8
    mate = seq + 1 - 2 * core
    lower = (rep + 7) % 8
    higher = (rep + 1) % 8
    me = 2 * half + core

    def dev(s):
        return (rep, s)

    def remote(src, dst, ss, rs, target):
        return pltpu.make_async_remote_copy(
            src_ref=src, dst_ref=dst, send_sem=ss, recv_sem=rs,
            device_id=target, device_id_type=MESH,
        )

    barrier = pltpu.get_barrier_semaphore()

    def greet(i, _):
        pl.semaphore_signal(barrier, inc=1, device_id=dev((seq + i) % 32), device_id_type=MESH)
        return 0

    own_rows = pl.ds(pl.multiple_of(core * TOK, TOK), TOK)
    loads = [
        pltpu.make_async_copy(k_hbm.at[0], kv_buf.at[0, own_rows, pl.ds(0, HD)], load_sem.at[0]),
        pltpu.make_async_copy(v_hbm.at[0], kv_buf.at[0, own_rows, pl.ds(HD, HD)], load_sem.at[1]),
        pltpu.make_async_copy(q_hbm.at[0], q_in, load_sem.at[2]),
        pltpu.make_async_copy(g_hbm.at[0], g_in, load_sem.at[3]),
        pltpu.make_async_copy(o_hbm.at[0], o_in, load_sem.at[4]),
        pltpu.make_async_copy(lse_hbm.at[0], lse_in, load_sem.at[5]),
        pltpu.make_async_copy(f_hbm.at[0], f_in, load_sem.at[6]),
        pltpu.make_async_copy(w_hbm.at[0], w_in, load_sem.at[7]),
    ]
    for load in loads:
        load.start()
    lax.fori_loop(1, 32, greet, 0)
    for other in (lower, higher):
        pl.semaphore_signal(barrier, inc=1, device_id=(other, seq), device_id_type=MESH)
    pl.semaphore_wait(barrier, 33)

    loads[0].wait()
    loads[1].wait()

    def kv_copy(j):
        return remote(
            kv_buf.at[0, own_rows, :], kv_buf.at[j, own_rows, :],
            kv_s.at[j], kv_r.at[j], dev(seq + 2 * j),
        )

    def forward(j):
        return remote(
            kv_buf.at[j, own_rows, :], kv_buf.at[j, own_rows, :],
            fw_s.at[j], fw_r.at[j], dev(mate),
        )

    forward(0).start()

    def kv_send(j, _):
        @pl.when(chip + j <= 15)
        def _():
            kv_copy(j).start()

        return 0

    lax.fori_loop(1, SPAN + 1, kv_send, 0)

    def x_slot(m, i):
        return x_all.at[
            pl.ds(pl.multiple_of(m * TOK, TOK), TOK), pl.ds(pl.multiple_of(i * ROWS, ROWS), ROWS)
        ]

    def x_copy(n, local):
        m, i = n // 4, n % 4
        block = 8 * (m // 2) + 2 * i + m % 2
        src = x_hbm.at[0, :, pl.ds(pl.multiple_of(block * ROWS, ROWS), ROWS)]
        if local:
            return pltpu.make_async_copy(src, x_slot(me, i), x_r.at[n])
        return remote(
            src, x_slot(me, i), x_s.at[n], x_r.at[4 * me + i],
            dev(16 * (m // 2) + 2 * zpos + m % 2),
        )

    def x_send(n, _):
        @pl.when(n // 4 == me)
        def _():
            x_copy(n, True).start()

        @pl.when(n // 4 != me)
        def _():
            x_copy(n, False).start()

        return 0

    lax.fori_loop(0, 16, x_send, 0)

    loads[2].wait()
    loads[3].wait()
    loads[4].wait()
    loads[5].wait()

    def prepare(h, _):
        lanes = pl.ds(pl.multiple_of(h * HD, HD), HD)
        q_h = q_in[:, lanes]
        g_h = g_in[:, lanes]
        q_rows[lanes, :] = q_h
        g_rows[lanes, :] = g_h
        q_cols[:, lanes] = q_h.T
        g_cols[:, lanes] = g_h.T
        delta = jnp.sum(g_h.astype(F32) * o_in[:, lanes].astype(F32), axis=1, keepdims=True)
        delta_b[lanes, :] = jnp.broadcast_to(delta, (TOK, HD))
        norm = lse_in[pl.ds(h, 1), :]
        lse_b[lanes, :] = jnp.broadcast_to(norm, (HD, TOK)).T
        return 0

    lax.fori_loop(0, HEADS, prepare, 0, unroll=2)

    loads[6].wait()
    loads[7].wait()
    acts[...] = lax.dot_general(f_in[...], w_in[...], NT, preferred_element_type=F32)
    acts_down = remote(acts, acts_in.at[1], a_s.at[0], a_r.at[1], (lower, seq))
    acts_up = remote(acts, acts_in.at[0], a_s.at[1], a_r.at[0], (higher, seq))
    acts_down.start()
    acts_up.start()
    contrib_down = remote(contrib.at[0], contrib_in.at[1], c_s.at[0], c_r.at[1], (lower, seq))
    contrib_up = remote(contrib.at[1], contrib_in.at[0], c_s.at[1], c_r.at[0], (higher, seq))

    def gossip():
        acts_down.wait()
        acts_up.wait()
        columns = []
        for k in range(4):
            mine = acts[k : k + 1, :]
            source = jnp.concatenate(
                [mine - acts_in[0, k : k + 1, :], mine - acts_in[1, k : k + 1, :]], axis=0
            )
            vector = source
            for previous in columns:
                vector = vector - jnp.mean(source * previous, axis=1, keepdims=True) * previous
            columns.append(
                vector * lax.rsqrt(jnp.mean(vector * vector, axis=1, keepdims=True) + EPS)
            )
        basis = jnp.concatenate(
            [columns[k][e : e + 1, :] for e in range(2) for k in range(4)], axis=0
        )
        left_out[0, 0] = basis[0:4]
        left_out[0, 1] = basis[4:8]
        both = jnp.dot(basis.astype(BF16), w_in[...], preferred_element_type=F32)
        contrib[0] = both[0:4]
        contrib[1] = both[4:8]
        contrib_down.start()
        contrib_up.start()

    last = jnp.minimum(chip, SPAN)
    scale = HD ** (-0.5)
    dq_acc[...] = jnp.zeros_like(dq_acc)

    def part_copy(j):
        return remote(part.at[j, 1 - core], pin.at[j], pt_s.at[j], pt_r.at[j], dev(mate))

    def grad_copy(j):
        return remote(gsend.at[j], grecv.at[j], gr_s.at[j], gr_r.at[j], dev(seq - 2 * j))

    def finish(j):
        part_copy(j).wait_recv()
        total = part[j, core] + pin[j]

        @pl.when(j == 0)
        def _():
            own[...] = total

        @pl.when(j > 0)
        def _():
            gsend[j] = total.astype(BF16)
            grad_copy(j).start()

    def step(j, _):
        @pl.when(j < last)
        def _():
            kv_copy(j + 1).wait_recv()
            forward(j + 1).start()

        forward(j).wait_recv()
        query_pos = core * TOK + lax.broadcasted_iota(jnp.int32, (TOK, 2 * TOK), 0)
        gap = lax.broadcasted_iota(jnp.int32, (TOK, 2 * TOK), 1) - query_pos
        seen = (gap <= 2 * TOK * j) & (gap > 2 * TOK * j - WINDOW)
        bias[...] = jnp.where(seen, 0.0, -1e30)
        keys = kv_buf[j, :, :HD]
        vals = kv_buf[j, :, HD:]
        scores = lax.dot_general(q_rows[...], keys, NT, preferred_element_type=F32)
        prob_grad = lax.dot_general(g_rows[...], vals, NT, preferred_element_type=F32)
        norm = lse_b[...]
        delta = delta_b[...]
        logits = scores * scale - jnp.concatenate([norm, norm], axis=1)
        logits = logits.reshape(HEADS, TOK, 2 * TOK) + bias[...][None]
        probs = jnp.exp(logits).reshape(HEADS * TOK, 2 * TOK)
        probs_b = probs.astype(BF16)
        diff = prob_grad - jnp.concatenate([delta, delta], axis=1)
        score_grad = (scale * probs * diff).astype(BF16)
        dq_acc[...] += jnp.dot(score_grad, keys, preferred_element_type=F32)
        value_grad = jnp.dot(g_cols[...], probs_b, preferred_element_type=F32)
        key_grad = jnp.dot(q_cols[...], score_grad, preferred_element_type=F32)
        for c in range(2):
            cols = slice(c * TOK, (c + 1) * TOK)
            part[j, c, :HD, :] = key_grad[:, cols]
            part[j, c, HD:, :] = value_grad[:, cols]
        part_copy(j).start()

        @pl.when(j == 0)
        def _():
            gossip()

        @pl.when(j > 0)
        def _():
            finish(j - 1)

        return 0

    lax.fori_loop(0, last + 1, step, 0)
    finish(last)

    def dq_copy(h):
        lanes = pl.ds(pl.multiple_of(h * HD, HD), HD)
        return pltpu.make_async_copy(dq_acc.at[lanes, :], dq_out.at[0, :, lanes], dq_s.at[h])

    def dq_send(h, _):
        dq_copy(h).start()
        return 0

    lax.fori_loop(0, HEADS, dq_send, 0)

    def gather_grad(j, _):
        @pl.when(chip + j <= 15)
        def _():
            grad_copy(j).wait_recv()
            own[...] += grecv[j].astype(F32)

        return 0

    lax.fori_loop(1, SPAN + 1, gather_grad, 0)
    kg[me] = own[...].astype(BF16)

    def kg_copy(m):
        return remote(
            kg.at[me], kg.at[me], kg_s.at[m], kg_r.at[me],
            dev(16 * (m // 2) + 2 * zpos + m % 2),
        )

    def kg_wait(m):
        return remote(
            kg.at[m], kg.at[m], kg_s.at[m], kg_r.at[m],
            dev(16 * (m // 2) + 2 * zpos + m % 2),
        )

    for m in range(4):
        @pl.when(me != m)
        def _():
            kg_copy(m).start()

    kv_out[0] = own[...].T

    contrib_down.wait()
    contrib_up.wait()
    right_out[0, 0] = contrib[...] + contrib_in[...]

    def x_wait(n, _):
        m, i = n // 4, n % 4

        @pl.when(m == me)
        def _():
            x_copy(n, True).wait()

        @pl.when(m != me)
        def _():
            remote(
                x_slot(m, i), x_slot(m, i), x_s.at[n], x_r.at[n],
                dev(16 * (m // 2) + 2 * zpos + m % 2),
            ).wait_recv()
            x_copy(n, False).wait_send()

        return 0

    lax.fori_loop(0, 16, x_wait, 0)
    for m in range(4):
        @pl.when(me != m)
        def _():
            kg_wait(m).wait_recv()

    def p_copy(i, c):
        return remote(
            psend.at[i, c], precv.at[zpos], pr_s.at[i, c], pr_r.at[zpos],
            dev(16 * half + 2 * (2 * i + core) + c),
        )

    lhs = jnp.concatenate([kg[m] for m in range(4)], axis=1)
    for i in range(4):
        term = jnp.dot(lhs, x_all[:, i * ROWS : (i + 1) * ROWS], preferred_element_type=F32)
        term = term.astype(BF16).T
        psend[i, 0] = term[:HALF]
        psend[i, 1] = term[HALF:]
        for c in range(2):
            @pl.when(16 * half + 2 * (2 * i + core) + c != seq)
            def _():
                p_copy(i, c).start()

    proj_out[0] = jnp.zeros((HALF, 2 * HD), F32)

    def p_add(z, _):
        source = 16 * half + 2 * z + zpos % 2

        @pl.when(source == seq)
        def _():
            proj_out[0] += psend[zpos // 2, core].astype(F32)

        @pl.when(source != seq)
        def _():
            remote(
                precv.at[z], precv.at[z], pr_s.at[0, 0], pr_r.at[z], dev(source)
            ).wait_recv()
            proj_out[0] += precv[z].astype(F32)

        return 0

    lax.fori_loop(0, 8, p_add, 0)

    def drain_kv(j, _):
        @pl.when((j > 0) & (chip + j <= 15))
        def _():
            kv_copy(j).wait_send()

        @pl.when(j <= last)
        def _():
            forward(j).wait_send()
            part_copy(j).wait_send()

        @pl.when((j > 0) & (j <= last))
        def _():
            grad_copy(j).wait_send()

        return 0

    lax.fori_loop(0, SPAN + 1, drain_kv, 0)
    for m in range(4):
        @pl.when(me != m)
        def _():
            kg_copy(m).wait_send()
    for i in range(4):
        for c in range(2):
            @pl.when(16 * half + 2 * (2 * i + core) + c != seq)
            def _():
                p_copy(i, c).wait_send()

    def dq_wait(h, _):
        dq_copy(h).wait()
        return 0

    lax.fori_loop(0, HEADS, dq_wait, 0)


def on_device(*args):
    any_spec = pl.BlockSpec(memory_space=pl.ANY)
    vmem = pl.BlockSpec(memory_space=pltpu.VMEM)
    dma = pltpu.SemaphoreType.DMA
    n = SPAN + 1
    rows = HEADS * TOK
    return pl.pallas_call(
        kernel,
        out_shape=(
            jax.ShapeDtypeStruct((1, TOK, HEADS * HD), F32),
            jax.ShapeDtypeStruct((1, TOK, 2 * HD), F32),
            jax.ShapeDtypeStruct((1, HALF, 2 * HD), F32),
            jax.ShapeDtypeStruct((1, 2, 4, ROWS), F32),
            jax.ShapeDtypeStruct((1, 1, 2, 4, 6144), F32),
        ),
        in_specs=[any_spec] * 9,
        out_specs=(any_spec, vmem, vmem, vmem, vmem),
        scratch_shapes=[
            pltpu.VMEM((TOK, HEADS * HD), BF16),
            pltpu.VMEM((TOK, HEADS * HD), BF16),
            pltpu.VMEM((TOK, HEADS * HD), BF16),
            pltpu.VMEM((HEADS, TOK), F32),
            pltpu.VMEM((ROWS, 6144), BF16),
            pltpu.VMEM((4, 6144), BF16),
            pltpu.VMEM((rows, HD), BF16),
            pltpu.VMEM((rows, HD), BF16),
            pltpu.VMEM((HD, rows), BF16),
            pltpu.VMEM((HD, rows), BF16),
            pltpu.VMEM((rows, HD), F32),
            pltpu.VMEM((rows, HD), F32),
            pltpu.VMEM((rows, HD), F32),
            pltpu.VMEM((TOK, 2 * TOK), F32),
            pltpu.VMEM((n, 2 * TOK, 2 * HD), BF16),
            pltpu.VMEM((n, 2, 2 * HD, TOK), F32),
            pltpu.VMEM((n, 2 * HD, TOK), F32),
            pltpu.VMEM((n, 2 * HD, TOK), BF16),
            pltpu.VMEM((n, 2 * HD, TOK), BF16),
            pltpu.VMEM((2 * HD, TOK), F32),
            pltpu.VMEM((4 * TOK, 4 * ROWS), BF16),
            pltpu.VMEM((4, 2 * HD, TOK), BF16),
            pltpu.VMEM((4, 2, HALF, 2 * HD), BF16),
            pltpu.VMEM((8, HALF, 2 * HD), BF16),
            pltpu.VMEM((4, ROWS), F32),
            pltpu.VMEM((2, 4, ROWS), F32),
            pltpu.VMEM((2, 4, 6144), F32),
            pltpu.VMEM((2, 4, 6144), F32),
            dma((8,)),
            dma((n,)), dma((n,)), dma((n,)), dma((n,)), dma((n,)), dma((n,)), dma((n,)), dma((n,)),
            dma((16,)), dma((16,)), dma((4,)), dma((4,)), dma((4, 2)), dma((8,)),
            dma((2,)), dma((2,)), dma((2,)), dma((2,)), dma((HEADS,)),
        ],
        compiler_params=pltpu.CompilerParams(
            collective_id=0, has_side_effects=True, vmem_limit_bytes=62 * 1024 * 1024
        ),
        name="fused",
    )(*args)


def solution(mesh):
    return jax.shard_map(
        on_device,
        mesh=mesh,
        in_specs=(
            P("rep", "seq", None),
            P("rep", "seq", None),
            P("rep", "seq", None),
            P("rep", "seq", None),
            P("rep", "seq", None),
            P("rep", None, "seq"),
            P("rep", "seq", None),
            P("rep", "seq", None),
            P("seq", None, None),
        ),
        out_specs=(
            P("rep", "seq", None),
            P("rep", "seq", None),
            P("rep", "seq", None),
            P("rep", None, None, "seq"),
            P("rep", "seq", None, None, None),
        ),
        check_vma=False,
    )
```

time: 390 us -> 78.5 us (0.20)
  the two profiles are of different devices: /device:TPU:1 before, /device:TPU:89 now
where the time goes in v1:
time: 78.5 us; the launch traced here: 78.4 us
  Pallas kernels  72.3 us (92%)
  local copies, waits for them, and re-layouts  5.38 us (7%)
    pallas_call x1, Pallas kernels, on_device(): pl.pallas_call(kernel, out_shape=(jax.ShapeDtypeStruct((1, TOK, HEADS * H...  72.3 us
    unnamed x13, local copies, waits for them, and re-layouts  5.38 us

profile of v1, /device:TPU:89, one launch (start us, length us, event | category | flops | bytes accessed | tf_op | source)
XLA Modules:
  0.0 78.4 jit_solution(14086781511908114839)
XLA Ops:
  0.6 72.3 %fused.1 = (f32[1,128,3072]{2,1,0:T(8,128)}, f32[1,128,256]{2,1,0:T(8,128)}, f32[1,192,256]{2,1,0:T(8,128)}, f32[1,2,4,384]{3,2,1,0:T(4,128)}, f32[1,1,2,4,6144]{4,3,2,1,0:T(4,128)}) custom-call(bf16[1,128,3072]{2,1,0:T(8,128)(2,1)} %q_hbm.1, bf16[1,128,128]{2,1,0:T(8,128)(2,1)} %k_hbm.1, bf16[1,128,128]{2,1,0:T(8,128)(2,1)} %v_hbm.1, ...), custom_call_target="tpu_custom_call" | custom-call | tf_op jit(solution)/shard_map/fused/pallas_call | solution.py:403
  73.0 0.0 copy-start.2
  73.0 0.0 copy-start.1
  73.0 0.0 copy-start.3
  73.0 0.0 copy-start
  73.0 2.8 %copy.19 = f32[1,128,3072]{2,1,0:T(8,128)} copy(f32[1,128,3072]{2,1,0:T(8,128)} %get-tuple-element.10) | data formatting | bytes 3145728
  75.8 0.0 copy-done.2
  75.8 0.7 copy.20
  76.4 0.0 copy-done.1
  76.4 0.7 copy.21
  77.1 0.0 copy-done.3
  77.1 0.6 copy.22
  77.7 0.0 copy-done
  77.7 0.7 copy.23
Async XLA Ops:
  73.0 2.8 %copy-start.2 = (f32[1,128,256]{2,1,0:T(8,128)S(1)}, f32[1,128,256]{2,1,0:T(8,128)}, u32[]{:S(2)}) copy-start(f32[1,128,256]{2,1,0:T(8,128)} %get-tuple-element.11) | copy-start | bytes 393220
  73.0 3.4 %copy-start.1 = (f32[1,192,256]{2,1,0:T(8,128)S(1)}, f32[1,192,256]{2,1,0:T(8,128)}, u32[]{:S(2)}) copy-start(f32[1,192,256]{2,1,0:T(8,128)} %get-tuple-element.12) | copy-start | bytes 589828
  73.0 4.1 %copy-start.3 = (f32[1,2,4,384]{3,2,1,0:T(4,128)S(1)}, f32[1,2,4,384]{3,2,1,0:T(4,128)}, u32[]{:S(2)}) copy-start(f32[1,2,4,384]{3,2,1,0:T(4,128)} %get-tuple-element.13) | copy-start | bytes 36868
  73.0 4.7 %copy-start = (f32[1,1,2,4,6144]{4,3,2,1,0:T(4,128)S(1)}, f32[1,1,2,4,6144]{4,3,2,1,0:T(4,128)}, u32[]{:S(2)}) copy-start(f32[1,1,2,4,6144]{4,3,2,1,0:T(4,128)} %get-tuple-element.14) | copy-start | bytes 589828

commit v2 on v1

--- a/solution.py
+++ b/solution.py
@@ -20,17 +20,21 @@
 ROWS = 384
 HALF = 192
 WINDOW = 2048
+ORDERS = ((1, 7, 3, 6, 5, 4, 2, 8), (1, 8, 7, 6, 3, 5, 4, 2))
+PIECES = 4
+PIECE = ROWS // PIECES
 
 
 def kernel(
     q_hbm, k_hbm, v_hbm, o_hbm, g_hbm, lse_hbm, x_hbm, w_hbm, f_hbm,
-    dq_out, kv_out, proj_out, left_out, right_out,
+    dq_acc, kv_out, proj_out, left_out, right_out,
     q_in, g_in, o_in, lse_in, w_in, f_in,
-    q_rows, g_rows, q_cols, g_cols, lse_b, delta_b, dq_acc, bias,
-    kv_buf, part, pin, gsend, grecv, own, x_all, kg, psend, precv,
+    q_rows, g_rows, q_cols, g_cols, lse_b, delta_b, bias,
+    kv_buf, part, pin, gsend, grecv, own, x_all, kg,
+    term, chain_out, chain_in, final_in, mate_in,
     acts, acts_in, contrib, contrib_in,
     load_sem, kv_s, kv_r, fw_s, fw_r, pt_s, pt_r, gr_s, gr_r,
-    x_s, x_r, kg_s, kg_r, pr_s, pr_r, a_s, a_r, c_s, c_r, dq_s,
+    x_s, x_r, kg_s, kg_r, ch_s, ch_r, fi_r, mt_s, mt_r, a_s, a_r, c_s, c_r,
 ):
     rep = lax.axis_index("rep")
     seq = lax.axis_index("seq")
@@ -74,6 +78,7 @@
     lax.fori_loop(1, 32, greet, 0)
     for other in (lower, higher):
         pl.semaphore_signal(barrier, inc=1, device_id=(other, seq), device_id_type=MESH)
+
     pl.semaphore_wait(barrier, 33)
 
     loads[0].wait()
@@ -93,14 +98,13 @@
 
     forward(0).start()
 
-    def kv_send(j, _):
+    def kv_send(j):
         @pl.when(chip + j <= 15)
         def _():
             kv_copy(j).start()
 
-        return 0
-
-    lax.fori_loop(1, SPAN + 1, kv_send, 0)
+    for j in (1, 8, 7, 6, 5):
+        kv_send(j)
 
     def x_slot(m, i):
         return x_all.at[
@@ -128,8 +132,6 @@
             x_copy(n, False).start()
 
         return 0
-
-    lax.fori_loop(0, 16, x_send, 0)
 
     loads[2].wait()
     loads[3].wait()
@@ -151,14 +153,11 @@
         return 0
 
     lax.fori_loop(0, HEADS, prepare, 0, unroll=2)
-
-    loads[6].wait()
-    loads[7].wait()
-    acts[...] = lax.dot_general(f_in[...], w_in[...], NT, preferred_element_type=F32)
+    kv_send(3)
+    lax.fori_loop(0, 16, x_send, 0)
+
     acts_down = remote(acts, acts_in.at[1], a_s.at[0], a_r.at[1], (lower, seq))
     acts_up = remote(acts, acts_in.at[0], a_s.at[1], a_r.at[0], (higher, seq))
-    acts_down.start()
-    acts_up.start()
     contrib_down = remote(contrib.at[0], contrib_in.at[1], c_s.at[0], c_r.at[1], (lower, seq))
     contrib_up = remote(contrib.at[1], contrib_in.at[0], c_s.at[1], c_r.at[0], (higher, seq))
 
@@ -189,6 +188,16 @@
         contrib_up.start()
 
     last = jnp.minimum(chip, SPAN)
+
+    def block_at(n):
+        block, before = 0, 1
+        for low, high in zip(*ORDERS):
+            j = jnp.where(half == 0, low, high)
+            held = j <= last
+            block = jnp.where(held & (before == n), j, block)
+            before = before + jnp.where(held, 1, 0)
+        return block
+
     scale = HD ** (-0.5)
     dq_acc[...] = jnp.zeros_like(dq_acc)
 
@@ -211,13 +220,25 @@
             gsend[j] = total.astype(BF16)
             grad_copy(j).start()
 
-    def step(j, _):
-        @pl.when(j < last)
-        def _():
-            kv_copy(j + 1).wait_recv()
-            forward(j + 1).start()
-
+    def pass_on(n):
+        @pl.when(n <= last)
+        def _():
+            kv_copy(block_at(n)).wait_recv()
+            forward(block_at(n)).start()
+
+    def step(n, _):
+        j = block_at(n)
+        pass_on(n + 1)
         forward(j).wait_recv()
+
+        @pl.when(n == jnp.minimum(1, last))
+        def _():
+            kv_send(4)
+
+        @pl.when(n == jnp.minimum(2, last))
+        def _():
+            kv_send(2)
+
         query_pos = core * TOK + lax.broadcasted_iota(jnp.int32, (TOK, 2 * TOK), 0)
         gap = lax.broadcasted_iota(jnp.int32, (TOK, 2 * TOK), 1) - query_pos
         seen = (gap <= 2 * TOK * j) & (gap > 2 * TOK * j - WINDOW)
@@ -243,28 +264,20 @@
             part[j, c, HD:, :] = value_grad[:, cols]
         part_copy(j).start()
 
-        @pl.when(j == 0)
-        def _():
-            gossip()
-
-        @pl.when(j > 0)
-        def _():
-            finish(j - 1)
+        @pl.when(n > 0)
+        def _():
+            finish(block_at(n - 1))
 
         return 0
 
     lax.fori_loop(0, last + 1, step, 0)
-    finish(last)
-
-    def dq_copy(h):
-        lanes = pl.ds(pl.multiple_of(h * HD, HD), HD)
-        return pltpu.make_async_copy(dq_acc.at[lanes, :], dq_out.at[0, :, lanes], dq_s.at[h])
-
-    def dq_send(h, _):
-        dq_copy(h).start()
-        return 0
-
-    lax.fori_loop(0, HEADS, dq_send, 0)
+    finish(block_at(last))
+
+    loads[6].wait()
+    loads[7].wait()
+    acts[...] = lax.dot_general(f_in[...], w_in[...], NT, preferred_element_type=F32)
+    acts_down.start()
+    acts_up.start()
 
     def gather_grad(j, _):
         @pl.when(chip + j <= 15)
@@ -277,28 +290,22 @@
     lax.fori_loop(1, SPAN + 1, gather_grad, 0)
     kg[me] = own[...].astype(BF16)
 
-    def kg_copy(m):
-        return remote(
-            kg.at[me], kg.at[me], kg_s.at[m], kg_r.at[me],
-            dev(16 * (m // 2) + 2 * zpos + m % 2),
-        )
-
-    def kg_wait(m):
-        return remote(
-            kg.at[m], kg.at[m], kg_s.at[m], kg_r.at[m],
-            dev(16 * (m // 2) + 2 * zpos + m % 2),
-        )
-
-    for m in range(4):
-        @pl.when(me != m)
-        def _():
-            kg_copy(m).start()
+    mate_m = 2 * half + 1 - core
+    over_m = 2 * (1 - half) + core
+    cross_m = 2 * (1 - half) + 1 - core
+    over = 16 * (1 - half) + 2 * zpos + core
+
+    def kg_copy(m, k, target):
+        return remote(kg.at[m], kg.at[m], kg_s.at[k], kg_r.at[m], dev(target))
+
+    kg_over = kg_copy(me, 0, over)
+    kg_mate = kg_copy(me, 1, mate)
+    kg_pass = kg_copy(over_m, 2, mate)
+    kg_over.start()
+    kg_mate.start()
 
     kv_out[0] = own[...].T
-
-    contrib_down.wait()
-    contrib_up.wait()
-    right_out[0, 0] = contrib[...] + contrib_in[...]
+    gossip()
 
     def x_wait(n, _):
         m, i = n // 4, n % 4
@@ -318,47 +325,90 @@
         return 0
 
     lax.fori_loop(0, 16, x_wait, 0)
-    for m in range(4):
-        @pl.when(me != m)
-        def _():
-            kg_wait(m).wait_recv()
-
-    def p_copy(i, c):
+    kg_copy(over_m, 2, mate).wait_recv()
+    kg_pass.start()
+    kg_copy(mate_m, 1, mate).wait_recv()
+    kg_copy(cross_m, 2, mate).wait_recv()
+
+    even = zpos % 2 == core
+    lhs = jnp.concatenate([kg[m] for m in range(4)], axis=1)
+
+    def place(z, c):
+        return dev(16 * half + 2 * (z % 8) + c)
+
+    def product(t):
+        ahead = jnp.where(even, (4, 6, 2, 0)[t], (5, 3, 7, 1)[t])
+        block = ((zpos + 8 - ahead) % 8) // 2
+        cols = pl.ds(pl.multiple_of(block * ROWS, ROWS), ROWS)
+        term[...] = jnp.dot(lhs, x_all[:, cols], preferred_element_type=F32).T
+
+    def hop(t, u, z):
         return remote(
-            psend.at[i, c], precv.at[zpos], pr_s.at[i, c], pr_r.at[zpos],
-            dev(16 * half + 2 * (2 * i + core) + c),
-        )
-
-    lhs = jnp.concatenate([kg[m] for m in range(4)], axis=1)
-    for i in range(4):
-        term = jnp.dot(lhs, x_all[:, i * ROWS : (i + 1) * ROWS], preferred_element_type=F32)
-        term = term.astype(BF16).T
-        psend[i, 0] = term[:HALF]
-        psend[i, 1] = term[HALF:]
-        for c in range(2):
-            @pl.when(16 * half + 2 * (2 * i + core) + c != seq)
-            def _():
-                p_copy(i, c).start()
-
-    proj_out[0] = jnp.zeros((HALF, 2 * HD), F32)
-
-    def p_add(z, _):
-        source = 16 * half + 2 * z + zpos % 2
-
-        @pl.when(source == seq)
-        def _():
-            proj_out[0] += psend[zpos // 2, core].astype(F32)
-
-        @pl.when(source != seq)
-        def _():
-            remote(
-                precv.at[z], precv.at[z], pr_s.at[0, 0], pr_r.at[z], dev(source)
-            ).wait_recv()
-            proj_out[0] += precv[z].astype(F32)
-
-        return 0
-
-    lax.fori_loop(0, 8, p_add, 0)
+            chain_out.at[t, u], chain_in.at[t, u], ch_s.at[t, u], ch_r.at[t, u], place(z, core)
+        )
+
+    def last_hop(t, u, side):
+        return remote(
+            chain_out.at[t, u], final_in.at[side, u % (PIECES // 2)],
+            ch_s.at[t, u], fi_r.at[side, u % (PIECES // 2)],
+            place(zpos + 9 - 2 * (1 - side), u // (PIECES // 2)),
+        )
+
+    def mate_hop():
+        rows = pl.ds(pl.multiple_of((1 - core) * HALF, HALF), HALF)
+        return remote(term.at[rows, :], mate_in, mt_s, mt_r, dev(mate))
+
+    towards = jnp.where(even, 7, 1)
+    backwards = jnp.where(even, 1, 7)
+    for t in range(4):
+        product(t)
+        for u in range(PIECES):
+            rows = slice(u * PIECE, (u + 1) * PIECE)
+            if t == 0:
+                chain_out[0, u] = term[rows, :].astype(BF16)
+                hop(0, u, zpos + towards).start()
+                continue
+            if t < 3:
+                hop(t - 1, u, zpos + backwards).wait_recv()
+                chain_out[t, u] = (term[rows, :] + chain_in[t - 1, u].astype(F32)).astype(BF16)
+            if t == 1:
+                hop(1, u, zpos + backwards).start()
+            if t == 2:
+                @pl.when(even)
+                def _():
+                    hop(2, u, zpos + 7).start()
+
+                @pl.when(jnp.logical_not(even))
+                def _():
+                    last_hop(2, u, 1).start()
+            if t == 3:
+                @pl.when(jnp.logical_not(even))
+                def _():
+                    hop(2, u, zpos + 1).wait_recv()
+                    chain_out[3, u] = (term[rows, :] + chain_in[2, u].astype(F32)).astype(BF16)
+                    last_hop(3, u, 0).start()
+
+    own_half = pl.ds(pl.multiple_of(core * HALF, HALF), HALF)
+
+    @pl.when(even)
+    def _():
+        mate_hop().start()
+        proj_out[0] = term[own_half, :]
+
+    contrib_down.wait()
+    contrib_up.wait()
+    right_out[0, 0] = contrib[...] + contrib_in[...]
+
+    @pl.when(jnp.logical_not(even))
+    def _():
+        mate_hop().wait_recv()
+        proj_out[0] = mate_in[...]
+
+    for side in (1, 0):
+        for v in range(PIECES // 2):
+            rows = slice(v * PIECE, (v + 1) * PIECE)
+            last_hop(2, v, side).wait_recv()
+            proj_out[0, rows, :] += final_in[side, v].astype(F32)
 
     def drain_kv(j, _):
         @pl.when((j > 0) & (chip + j <= 15))
@@ -377,21 +427,38 @@
         return 0
 
     lax.fori_loop(0, SPAN + 1, drain_kv, 0)
-    for m in range(4):
-        @pl.when(me != m)
-        def _():
-            kg_copy(m).wait_send()
-    for i in range(4):
-        for c in range(2):
-            @pl.when(16 * half + 2 * (2 * i + core) + c != seq)
-            def _():
-                p_copy(i, c).wait_send()
-
-    def dq_wait(h, _):
-        dq_copy(h).wait()
-        return 0
-
-    lax.fori_loop(0, HEADS, dq_wait, 0)
+    kg_over.wait_send()
+    kg_mate.wait_send()
+    kg_pass.wait_send()
+    for u in range(PIECES):
+        for t in range(3):
+            hop(t, u, zpos + 1).wait_send()
+
+        @pl.when(jnp.logical_not(even))
+        def _():
+            last_hop(3, u, 0).wait_send()
+
+    @pl.when(even)
+    def _():
+        mate_hop().wait_send()
+
+
+def emit(dq, kv, proj, left, right, dq_out, kv_out, proj_out, left_out, right_out, sem, head_sem):
+    copies = [
+        pltpu.make_async_copy(src, dst, sem.at[k])
+        for k, (src, dst) in enumerate(
+            ((kv, kv_out), (proj, proj_out), (left, left_out), (right, right_out))
+        )
+    ]
+    for h in range(HEADS):
+        lanes = slice(h * HD, (h + 1) * HD)
+        copies.append(
+            pltpu.make_async_copy(dq.at[lanes, :], dq_out.at[0, :, lanes], head_sem.at[h])
+        )
+    for copy in copies:
+        copy.start()
+    for copy in copies:
+        copy.wait()
 
 
 def on_device(*args):
@@ -400,17 +467,17 @@
     dma = pltpu.SemaphoreType.DMA
     n = SPAN + 1
     rows = HEADS * TOK
-    return pl.pallas_call(
+    results = pl.pallas_call(
         kernel,
         out_shape=(
-            jax.ShapeDtypeStruct((1, TOK, HEADS * HD), F32),
-            jax.ShapeDtypeStruct((1, TOK, 2 * HD), F32),
-            jax.ShapeDtypeStruct((1, HALF, 2 * HD), F32),
-            jax.ShapeDtypeStruct((1, 2, 4, ROWS), F32),
-            jax.ShapeDtypeStruct((1, 1, 2, 4, 6144), F32),
+            pltpu.VMEM((rows, HD), F32),
+            pltpu.VMEM((1, TOK, 2 * HD), F32),
+            pltpu.VMEM((1, HALF, 2 * HD), F32),
+            pltpu.VMEM((1, 2, 4, ROWS), F32),
+            pltpu.VMEM((1, 1, 2, 4, 6144), F32),
         ),
         in_specs=[any_spec] * 9,
-        out_specs=(any_spec, vmem, vmem, vmem, vmem),
+        out_specs=(vmem,) * 5,
         scratch_shapes=[
             pltpu.VMEM((TOK, HEADS * HD), BF16),
             pltpu.VMEM((TOK, HEADS * HD), BF16),
@@ -424,7 +491,6 @@
             pltpu.VMEM((HD, rows), BF16),
             pltpu.VMEM((rows, HD), F32),
             pltpu.VMEM((rows, HD), F32),
-            pltpu.VMEM((rows, HD), F32),
             pltpu.VMEM((TOK, 2 * TOK), F32),
             pltpu.VMEM((n, 2 * TOK, 2 * HD), BF16),
             pltpu.VMEM((n, 2, 2 * HD, TOK), F32),
@@ -434,22 +500,41 @@
             pltpu.VMEM((2 * HD, TOK), F32),
             pltpu.VMEM((4 * TOK, 4 * ROWS), BF16),
             pltpu.VMEM((4, 2 * HD, TOK), BF16),
-            pltpu.VMEM((4, 2, HALF, 2 * HD), BF16),
-            pltpu.VMEM((8, HALF, 2 * HD), BF16),
+            pltpu.VMEM((ROWS, 2 * HD), F32),
+            pltpu.VMEM((4, PIECES, PIECE, 2 * HD), BF16),
+            pltpu.VMEM((3, PIECES, PIECE, 2 * HD), BF16),
+            pltpu.VMEM((2, PIECES // 2, PIECE, 2 * HD), BF16),
+            pltpu.VMEM((HALF, 2 * HD), F32),
             pltpu.VMEM((4, ROWS), F32),
             pltpu.VMEM((2, 4, ROWS), F32),
             pltpu.VMEM((2, 4, 6144), F32),
             pltpu.VMEM((2, 4, 6144), F32),
             dma((8,)),
             dma((n,)), dma((n,)), dma((n,)), dma((n,)), dma((n,)), dma((n,)), dma((n,)), dma((n,)),
-            dma((16,)), dma((16,)), dma((4,)), dma((4,)), dma((4, 2)), dma((8,)),
-            dma((2,)), dma((2,)), dma((2,)), dma((2,)), dma((HEADS,)),
+            dma((16,)), dma((16,)), dma((3,)), dma((4,)),
+            dma((4, PIECES)), dma((3, PIECES)), dma((2, PIECES // 2)), dma, dma,
+            dma((2,)), dma((2,)), dma((2,)), dma((2,)),
         ],
         compiler_params=pltpu.CompilerParams(
-            collective_id=0, has_side_effects=True, vmem_limit_bytes=62 * 1024 * 1024
+            collective_id=0, has_side_effects=True, vmem_limit_bytes=56 * 1024 * 1024
         ),
         name="fused",
     )(*args)
+    return pl.pallas_call(
+        emit,
+        out_shape=(
+            jax.ShapeDtypeStruct((1, TOK, HEADS * HD), F32),
+            jax.ShapeDtypeStruct((1, TOK, 2 * HD), F32),
+            jax.ShapeDtypeStruct((1, HALF, 2 * HD), F32),
+            jax.ShapeDtypeStruct((1, 2, 4, ROWS), F32),
+            jax.ShapeDtypeStruct((1, 1, 2, 4, 6144), F32),
+        ),
+        in_specs=[vmem] * 5,
+        out_specs=(any_spec,) * 5,
+        scratch_shapes=[dma((4,)), dma((HEADS,))],
+        compiler_params=pltpu.CompilerParams(vmem_limit_bytes=4 * 1024 * 1024),
+        name="emit",
+    )(*results)
 
 
 def solution(mesh):

time: 78.5 us -> 68.8 us (0.88)
  the two profiles are of different devices: /device:TPU:89 before, /device:TPU:1 now
where the time goes in v2:
time: 68.8 us; the launch traced here: 68.4 us
  Pallas kernels  67.8 us (99%)
    pallas_call x1, Pallas kernels, on_device(): pl.pallas_call(kernel, out_shape=(pltpu.VMEM((rows, HD), F32), pltpu.VMEM...  66.2 us
    pallas_call x1, Pallas kernels, on_device(): pl.pallas_call(emit, out_shape=(jax.ShapeDtypeStruct((1, TOK, HEADS * HD)...  1.56 us

profile of v2, /device:TPU:1, one launch (start us, length us, event | category | flops | bytes accessed | tf_op | source)
XLA Modules:
  0.0 68.4 jit_solution(1377211396938961655)
XLA Ops:
  0.6 66.2 %fused.1 = (f32[3072,128]{1,0:T(8,128)S(1)}, f32[1,128,256]{2,1,0:T(8,128)S(1)}, f32[1,192,256]{2,1,0:T(8,128)S(1)}, f32[1,2,4,384]{3,2,1,0:T(4,128)S(1)}, f32[1,1,2,4,6144]{4,3,2,1,0:T(4,128)S(1)}) custom-call(bf16[1,128,3072]{2,1,0:T(8,128)(2,1)} %q_hbm.1, bf16[1,128,128]{2,1,0:T(8,128)(2,1)} %k_hbm.1, bf16[1,128,128]{2,1,0:T(8,128)(2,1)} %v_hbm.1, ...), custom_call_target="tpu_custom_call" | custom-call | tf_op jit(solution)/shard_map/fused/pallas_call | solution.py:470
  66.8 1.6 %emit.1 = (f32[1,128,3072]{2,1,0:T(8,128)}, f32[1,128,256]{2,1,0:T(8,128)}, f32[1,192,256]{2,1,0:T(8,128)}, f32[1,2,4,384]{3,2,1,0:T(4,128)}, f32[1,1,2,4,6144]{4,3,2,1,0:T(4,128)}) custom-call(f32[3072,128]{1,0:T(8,128)S(1)} %get-tuple-element.10.dq, f32[1,128,256]{2,1,0:T(8,128)S(1)} %get-tuple-element.11.kv, f32[1,192,256]{2,1,0:T(8,128)S(1)} %get-tuple-element.12.proj, ...), custom_call_target="tpu_custom_call" | custom-call | tf_op jit(solution)/shard_map/emit/pallas_call | solution.py:523

commit v3 on v2

--- a/solution.py
+++ b/solution.py
@@ -20,8 +20,8 @@
 ROWS = 384
 HALF = 192
 WINDOW = 2048
-ORDERS = ((1, 7, 3, 6, 5, 4, 2, 8), (1, 8, 7, 6, 3, 5, 4, 2))
-PIECES = 4
+ORDERS = ((5, 3, 4, 6, 7, 2, 1, 8), (8, 5, 3, 4, 6, 2, 7, 1))
+PIECES = 6
 PIECE = ROWS // PIECES
 
 
@@ -33,7 +33,7 @@
     kv_buf, part, pin, gsend, grecv, own, x_all, kg,
     term, chain_out, chain_in, final_in, mate_in,
     acts, acts_in, contrib, contrib_in,
-    load_sem, kv_s, kv_r, fw_s, fw_r, pt_s, pt_r, gr_s, gr_r,
+    load_sem, kv_s, kv_r, sp_s, fw_s, fw_r, pt_s, pt_r, gr_s, gr_r,
     x_s, x_r, kg_s, kg_r, ch_s, ch_r, fi_r, mt_s, mt_r, a_s, a_r, c_s, c_r,
 ):
     rep = lax.axis_index("rep")
@@ -99,11 +99,21 @@
     forward(0).start()
 
     def kv_send(j):
-        @pl.when(chip + j <= 15)
+        held = chip + j <= 15
+        if j in (6, 7):
+            held = zpos + j <= 7
+
+        @pl.when(held)
         def _():
             kv_copy(j).start()
 
-    for j in (1, 8, 7, 6, 5):
+    def spread(j):
+        return remote(
+            kv_buf.at[SPAN, own_rows, :], kv_buf.at[j, own_rows, :],
+            sp_s.at[j - 5], kv_r.at[j], dev(seq + 2 * (j - SPAN)),
+        )
+
+    for j in (8, 5, 3, 4, 6, 7, 2, 1):
         kv_send(j)
 
     def x_slot(m, i):
@@ -153,7 +163,6 @@
         return 0
 
     lax.fori_loop(0, HEADS, prepare, 0, unroll=2)
-    kv_send(3)
     lax.fori_loop(0, 16, x_send, 0)
 
     acts_down = remote(acts, acts_in.at[1], a_s.at[0], a_r.at[1], (lower, seq))
@@ -226,18 +235,17 @@
             kv_copy(block_at(n)).wait_recv()
             forward(block_at(n)).start()
 
+        @pl.when((half == 1) & (n == 1))
+        def _():
+            for j in (6, 7):
+                @pl.when(zpos + j >= SPAN)
+                def _():
+                    spread(j).start()
+
     def step(n, _):
         j = block_at(n)
         pass_on(n + 1)
         forward(j).wait_recv()
-
-        @pl.when(n == jnp.minimum(1, last))
-        def _():
-            kv_send(4)
-
-        @pl.when(n == jnp.minimum(2, last))
-        def _():
-            kv_send(2)
 
         query_pos = core * TOK + lax.broadcasted_iota(jnp.int32, (TOK, 2 * TOK), 0)
         gap = lax.broadcasted_iota(jnp.int32, (TOK, 2 * TOK), 1) - query_pos
@@ -411,7 +419,9 @@
             proj_out[0, rows, :] += final_in[side, v].astype(F32)
 
     def drain_kv(j, _):
-        @pl.when((j > 0) & (chip + j <= 15))
+        spread_by = (j >= 6) & (j <= 7)
+
+        @pl.when((j > 0) & jnp.where(spread_by, zpos + j <= 7, chip + j <= 15))
         def _():
             kv_copy(j).wait_send()
 
@@ -427,6 +437,11 @@
         return 0
 
     lax.fori_loop(0, SPAN + 1, drain_kv, 0)
+    for j in (6, 7):
+        @pl.when((half == 1) & (zpos + j >= SPAN))
+        def _():
+            spread(j).wait_send()
+
     kg_over.wait_send()
     kg_mate.wait_send()
     kg_pass.wait_send()
@@ -510,7 +525,7 @@
             pltpu.VMEM((2, 4, 6144), F32),
             pltpu.VMEM((2, 4, 6144), F32),
             dma((8,)),
-            dma((n,)), dma((n,)), dma((n,)), dma((n,)), dma((n,)), dma((n,)), dma((n,)), dma((n,)),
+            dma((n,)), dma((n,)), dma((3,)), dma((n,)), dma((n,)), dma((n,)), dma((n,)), dma((n,)), dma((n,)),
             dma((16,)), dma((16,)), dma((3,)), dma((4,)),
             dma((4, PIECES)), dma((3, PIECES)), dma((2, PIECES // 2)), dma, dma,
             dma((2,)), dma((2,)), dma((2,)), dma((2,)),

time: 68.8 us -> 67.8 us (0.985)
  Pallas kernels: 67.8 us -> 67.1 us
where the time goes in v3:
time: 67.8 us; the launch traced here: 67.7 us
  Pallas kernels  67.1 us (99%)
    pallas_call x1, Pallas kernels, on_device(): pl.pallas_call(kernel, out_shape=(pltpu.VMEM((rows, HD), F32), pltpu.VMEM...  65.5 us
    pallas_call x1, Pallas kernels, on_device(): pl.pallas_call(emit, out_shape=(jax.ShapeDtypeStruct((1, TOK, HEADS * HD)...  1.56 us

profile of v3, /device:TPU:1, one launch (start us, length us, event | category | flops | bytes accessed | tf_op | source)
XLA Modules:
  0.0 67.7 jit_solution(14048093443029049077)
XLA Ops:
  0.6 65.5 %fused.1 = (f32[3072,128]{1,0:T(8,128)S(1)}, f32[1,128,256]{2,1,0:T(8,128)S(1)}, f32[1,192,256]{2,1,0:T(8,128)S(1)}, f32[1,2,4,384]{3,2,1,0:T(4,128)S(1)}, f32[1,1,2,4,6144]{4,3,2,1,0:T(4,128)S(1)}) custom-call(bf16[1,128,3072]{2,1,0:T(8,128)(2,1)} %q_hbm.1, bf16[1,128,128]{2,1,0:T(8,128)(2,1)} %k_hbm.1, bf16[1,128,128]{2,1,0:T(8,128)(2,1)} %v_hbm.1, ...), custom_call_target="tpu_custom_call" | custom-call | tf_op jit(solution)/shard_map/fused/pallas_call | solution.py:485
  66.2 1.6 %emit.1 = (f32[1,128,3072]{2,1,0:T(8,128)}, f32[1,128,256]{2,1,0:T(8,128)}, f32[1,192,256]{2,1,0:T(8,128)}, f32[1,2,4,384]{3,2,1,0:T(4,128)}, f32[1,1,2,4,6144]{4,3,2,1,0:T(4,128)}) custom-call(f32[3072,128]{1,0:T(8,128)S(1)} %get-tuple-element.10.dq, f32[1,128,256]{2,1,0:T(8,128)S(1)} %get-tuple-element.11.kv, f32[1,192,256]{2,1,0:T(8,128)S(1)} %get-tuple-element.12.proj, ...), custom_call_target="tpu_custom_call" | custom-call | tf_op jit(solution)/shard_map/emit/pallas_call | solution.py:538
